TPU v7x, 128 devices: a whole 4x4x4 slice. The times are simulated.
128 devices in a mesh: tok: 16 (over x_hi, z, core), wid: 8 (over y, x_lo).
Axes of the slice: x: 4 (x_hi: 2, x_lo: 2; x = x_hi * 2 + x_lo), y: 4, z: 4, core: 2. Of those that a mesh axis runs over, the one named last changes fastest.
Arguments:
- tokens: bfloat16 [9344, 1024], P('tok', 'wid'), may hold values from -6 to 6
- image_ids: int32 [9344], P('tok'), may hold values from 1 to 9360, as said below
- norm_gains: float32 [2, 2, 1024], P(None, None, 'wid'), may hold values from 0.5 to 1.5
- norm_shifts: float32 [2, 2, 1024], P(None, None, 'wid'), may hold values from -1.8 to 1.8
- qkv_weight: bfloat16 [2, 1024, 3, 1024], P(None, 'tok', None, 'wid'), may hold values from -0.1875 to 0.1875
- qv_bias: float32 [2, 2, 1024], P(None, None, 'wid'), may hold values from -3 to 3
- out_weight: bfloat16 [2, 1024, 1024], P(None, 'wid', 'tok'), may hold values from -0.75 to 0.75
- out_bias: float32 [2, 1024], P(None, 'wid'), may hold values from -3 to 3
- up_weight: bfloat16 [2, 1024, 4096], P(None, 'tok', 'wid'), may hold values from -0.1875 to 0.1875
- up_bias: float32 [2, 4096], P(None, 'wid'), may hold values from -3 to 3
- down_weight: bfloat16 [2, 4096, 1024], P(None, 'wid', 'tok'), may hold values from -0.125 to 0.125
- down_bias: float32 [2, 1024], P(None, 'wid'), may hold values from -3 to 3
- out_grad: bfloat16 [9344, 1024], P('tok', 'wid'), may hold values from -6 to 6
Outputs:
- activations: bfloat16 [9344, 1024], P('tok', 'wid')
- input_grad: float32 [9344, 1024], P('tok', 'wid')
- gain_grad: float32 [2, 2, 1024], P(None, None, 'wid')
- shift_grad: float32 [2, 2, 1024], P(None, None, 'wid')
- qkv_grad: float32 [2, 1024, 3, 1024], P(None, 'tok', None, 'wid')
- qv_bias_grad: float32 [2, 2, 1024], P(None, None, 'wid')
- out_weight_grad: float32 [2, 1024, 1024], P(None, 'wid', 'tok')
- out_bias_grad: float32 [2, 1024], P(None, 'wid')
- up_weight_grad: float32 [2, 1024, 4096], P(None, 'tok', 'wid')
- up_bias_grad: float32 [2, 4096], P(None, 'wid')
- down_weight_grad: float32 [2, 4096, 1024], P(None, 'wid', 'tok')
- down_bias_grad: float32 [2, 1024], P(None, 'wid')
Inputs may be any that keep to these rules, and one draw needn't show every extreme that they name: `image_ids`: images 1 to 16, in order, each hold exactly 577 consecutive tokens; each aligned block of 584 tokens holds one whole image; every other token has a number of its own above 16, and the last token of each block is such a token.
All inputs are finite; a program needn't handle non-finite values.
Results may differ from a plain program's by a relative error of at most 0.02.
Values may be sent and summed in bfloat16 or wider, within the bound.
No kernel may reach another device: no remote copies, remote signals or barrier semaphores. Data moves between devices by JAX's collectives and lax.ppermute only.
A program may use at most 128 MiB of HBM per device.

v0:
```python
import jax
import jax.numpy as jnp
from jax import lax
from jax.sharding import PartitionSpec as P

HEAD = 64
LAYERS = 2
EPSILON = 1e-06


def copy_for_each(value, axis):
    copies = jnp.broadcast_to(value, (lax.axis_size(axis), *value.shape))
    return lax.all_to_all(copies, axis, split_axis=0, concat_axis=0, tiled=True)


def over_copies(value, axis):
    everything = copy_for_each(value, axis)
    return jnp.sum(everything, axis=0)


def in_one(arrays, axis):
    line, at, finished = (jnp.concatenate([a.reshape(-1) for a in arrays]), 0, [])
    so_far = over_copies(line, axis)
    for a in arrays:
        finished.append(so_far[at : at + a.size].reshape(a.shape))
        at += a.size
    return tuple(finished)


def in_order(tiles, dim):
    dims = list(tiles.shape[1:])
    dims[dim] *= tiles.shape[0]
    return jnp.moveaxis(tiles, 0, dim).reshape(dims)


def collect(value, axis, dim):
    tiles = copy_for_each(value, axis)
    return in_order(tiles, dim)


def cut_along(value, dim, peers):
    before, after = (value.shape[:dim], value.shape[dim + 1 :])
    return jnp.moveaxis(value.reshape(*before, peers, -1, *after), dim, 0)


def summed_on_arrival(value, axis, dim):
    tiles = cut_along(value, dim, lax.axis_size(axis))
    arrived = lax.all_to_all(tiles, axis, split_axis=0, concat_axis=0, tiled=True)
    return arrived.astype(jnp.float32).sum(axis=0)


def turned_gather(arrays, axis, dims):
    turned = [jnp.moveaxis(a, dim, 0) for a, dim in zip(arrays, dims)]
    both = jnp.concatenate([t.reshape(len(t), -1) for t in turned], axis=1)
    filled, at, finished = (lax.all_gather(both, axis, axis=0, tiled=True), 0, [])
    for t, dim in zip(turned, dims):
        piece = filled[:, at : at + t[0].size].reshape(-1, *t.shape[1:])
        finished.append(jnp.moveaxis(piece, 0, dim))
        at += t[0].size
    return tuple(finished)


def sum_together(arrays, axis, dims):
    peers = lax.axis_size(axis)
    tiles = [cut_along(a, dim, peers) for a, dim in zip(arrays, dims)]
    lines = jnp.concatenate([b.reshape(peers, -1) for b in tiles], axis=1)
    span = max(16, -(-lines.shape[1] // 1024) * 8)
    lines = jnp.pad(lines, ((0, 0), (0, span * 128 - lines.shape[1]))).reshape(-1, 128)
    line, at, finished = (lax.psum_scatter(lines, axis, tiled=True).reshape(-1), 0, [])
    for b in tiles:
        part = b[0]
        finished.append(line[at : at + part.size].reshape(part.shape))
        at += part.size
    return tuple(finished)


def contract_rows(left, right):
    return lax.dot_general(
        left, right, (((0,), (0,)), ((), ())), preferred_element_type=jnp.float32
    )


def contract_cols(left, right):
    return lax.dot_general(
        left, right, (((1,), (1,)), ((), ())), preferred_element_type=jnp.float32
    )


def norm_forward(values, gain, shift, width):
    totals = in_one((jnp.sum(values, axis=1), jnp.sum(values * values, axis=1)), "wid")
    mean = totals[0] / width
    spread = totals[1] / width - mean * mean
    row_scale = lax.rsqrt(spread + EPSILON)
    centred = (values - mean[:, None]) * row_scale[:, None]
    return (centred, row_scale, centred * gain + shift)


def norm_backward(dnormed, centred, row_scale, gain, width):
    scaled = dnormed * gain
    totals = in_one((jnp.sum(scaled, axis=1), jnp.sum(scaled * centred, axis=1)), "wid")
    dvalues = row_scale[:, None] * (
        scaled - totals[0][:, None] / width - centred * (totals[1][:, None] / width)
    )
    return (dvalues, jnp.sum(dnormed * centred, axis=0), jnp.sum(dnormed, axis=0))


def full_rows(values):
    return collect(values, "wid", 1)


def width_sum(partial_value):
    return summed_on_arrival(partial_value.astype(jnp.bfloat16), "wid", 1)


def split_heads(values, heads):
    return values.reshape(values.shape[0], heads, values.shape[1] // heads)


def scores_of(query, keys, token_ids, heads):
    raw = jnp.einsum(
        "qhe,khe->hqk",
        split_heads(query, heads),
        split_heads(keys, heads),
        preferred_element_type=jnp.float32,
    )
    allowed = token_ids[:, None] == token_ids[None, :]
    return jnp.where(allowed[None], raw * HEAD ** (-0.5), -1e30)


def attend(query, keys, values, token_ids, heads):
    scores = scores_of(query, keys, token_ids, heads)
    top = jnp.max(scores, axis=2, keepdims=True)
    expo = jnp.exp(scores - top)
    total = jnp.sum(expo, axis=2, keepdims=True)
    probs = (expo / total).astype(jnp.bfloat16)
    mixed = jnp.einsum(
        "hqk,khe->qhe", probs, split_heads(values, heads), preferred_element_type=jnp.float32
    )
    return (mixed.reshape(query.shape[0], query.shape[1]), top + jnp.log(total))


def attend_back(dmixed, query, keys, values, token_ids, logsum, heads):
    scores = scores_of(query, keys, token_ids, heads)
    probs = jnp.exp(scores - logsum)
    dmix3 = split_heads(dmixed, heads)
    dvalues = jnp.einsum(
        "hqk,qhe->khe", probs.astype(jnp.bfloat16), dmix3, preferred_element_type=jnp.float32
    )
    dprobs = jnp.einsum(
        "qhe,khe->hqk", dmix3, split_heads(values, heads), preferred_element_type=jnp.float32
    )
    centre = jnp.sum(probs * dprobs, axis=2, keepdims=True)
    dscores = (probs * (dprobs - centre)).astype(jnp.bfloat16)
    scale = HEAD ** (-0.5)
    dquery = (
        jnp.einsum(
            "hqk,khe->qhe", dscores, split_heads(keys, heads), preferred_element_type=jnp.float32
        )
        * scale
    )
    dkeys = (
        jnp.einsum(
            "hqk,qhe->khe", dscores, split_heads(query, heads), preferred_element_type=jnp.float32
        )
        * scale
    )
    rows = query.shape[0]
    return (dquery.reshape(rows, -1), dkeys.reshape(rows, -1), dvalues.reshape(rows, -1))


def gelu_slope(pre):
    return (
        0.5 * (1.0 + lax.erf(pre * 0.7071067811865476))
        + pre * jnp.exp(-0.5 * pre * pre) * 0.3989422804014327
    )


def shards(
    tokens,
    image_ids,
    norm_gains,
    norm_shifts,
    qkv_weight,
    qv_bias,
    out_weight,
    out_bias,
    up_weight,
    up_bias,
    down_weight,
    down_bias,
    out_grad,
):
    rows = tokens.shape[0]
    cols = tokens.shape[1]
    width = cols * lax.axis_size("wid")
    heads = cols // HEAD
    state = tokens.astype(jnp.float32)
    kept = []
    saved = []
    for layer in range(LAYERS):
        matrices = turned_gather(
            (qkv_weight[layer], out_weight[layer], up_weight[layer], down_weight[layer]),
            "tok",
            (0, 1, 0, 1),
        )
        qkv_full, out_full, up_full, down_full = matrices
        kept.append(matrices)
        centred1, scale1, normed1 = norm_forward(
            state, norm_gains[layer, 0], norm_shifts[layer, 0], width
        )
        rows1 = full_rows(normed1.astype(jnp.bfloat16))
        proj = jnp.dot(
            rows1, qkv_full.reshape(width, 3 * cols), preferred_element_type=jnp.float32
        ).reshape(rows, 3, cols)
        query = (proj[:, 0] + qv_bias[layer, 0]).astype(jnp.bfloat16)
        keys = proj[:, 1].astype(jnp.bfloat16)
        values = (proj[:, 2] + qv_bias[layer, 1]).astype(jnp.bfloat16)
        mixed, logsum = attend(query, keys, values, image_ids, heads)
        attended = mixed.astype(jnp.bfloat16)
        branch = width_sum(jnp.dot(attended, out_full, preferred_element_type=jnp.float32))
        middle = state + branch + out_bias[layer]
        centred2, scale2, normed2 = norm_forward(
            middle, norm_gains[layer, 1], norm_shifts[layer, 1], width
        )
        rows2 = full_rows(normed2.astype(jnp.bfloat16))
        pre = jnp.dot(rows2, up_full, preferred_element_type=jnp.float32) + up_bias[layer]
        hidden = jax.nn.gelu(pre, approximate=False).astype(jnp.bfloat16)
        state = (
            middle
            + width_sum(jnp.dot(hidden, down_full, preferred_element_type=jnp.float32))
            + down_bias[layer]
        )
        saved.append(
            (
                centred1,
                scale1,
                rows1,
                query,
                keys,
                values,
                logsum,
                attended,
                centred2,
                scale2,
                rows2,
                pre,
                hidden,
            )
        )
    activations = state.astype(jnp.bfloat16)
    grad_state = out_grad.astype(jnp.float32)
    results = []
    for layer in reversed(range(LAYERS)):
        matrices = turned_gather(
            (qkv_weight[layer], out_weight[layer], up_weight[layer], down_weight[layer]),
            "tok",
            (0, 1, 0, 1),
        )
        qkv_full, out_full, up_full, down_full = matrices
        (
            centred1,
            scale1,
            rows1,
            query,
            keys,
            values,
            logsum,
            attended,
            centred2,
            scale2,
            rows2,
            pre,
            hidden,
        ) = saved[layer]
        grad_branch = grad_state.astype(jnp.bfloat16)
        grad_rows = full_rows(grad_branch)
        dhidden = contract_cols(grad_rows, down_full)
        ddown = contract_rows(hidden, grad_rows)
        dpre = (dhidden * gelu_slope(pre)).astype(jnp.bfloat16)
        dup = contract_rows(rows2, dpre)
        dnormed2 = width_sum(contract_cols(dpre, up_full))
        dmiddle, dgain2, dshift2 = norm_backward(
            dnormed2, centred2, scale2, norm_gains[layer, 1], width
        )
        grad_middle = grad_state + dmiddle
        grad_attn = grad_middle.astype(jnp.bfloat16)
        attn_rows = full_rows(grad_attn)
        dmixed = contract_cols(attn_rows, out_full).astype(jnp.bfloat16)
        dout = contract_rows(attended, attn_rows)
        dquery, dkeys, dvalues = attend_back(dmixed, query, keys, values, image_ids, logsum, heads)
        dquery = dquery.astype(jnp.bfloat16)
        dkeys = dkeys.astype(jnp.bfloat16)
        dvalues = dvalues.astype(jnp.bfloat16)
        dproj = jnp.stack([dquery, dkeys, dvalues], axis=1).reshape(rows, 3 * cols)
        dqkv = contract_rows(rows1, dproj).reshape(width, 3, cols)
        dnormed1 = width_sum(contract_cols(dproj, qkv_full.reshape(width, 3 * cols)))
        dinput, dgain1, dshift1 = norm_backward(
            dnormed1, centred1, scale1, norm_gains[layer, 0], width
        )
        grad_state = grad_middle + dinput
        weight_parts = tuple(
            (
                part.astype(jnp.float32)
                for part in sum_together(
                    (
                        dqkv.astype(jnp.bfloat16),
                        dout.astype(jnp.bfloat16),
                        dup.astype(jnp.bfloat16),
                        ddown.astype(jnp.bfloat16),
                    ),
                    "tok",
                    (0, 1, 0, 1),
                )
            )
        )
        vector_parts = in_one(
            (
                jnp.stack([dgain1, dgain2]),
                jnp.stack([dshift1, dshift2]),
                jnp.stack(
                    [
                        jnp.sum(dquery, axis=0, dtype=jnp.float32),
                        jnp.sum(dvalues, axis=0, dtype=jnp.float32),
                    ]
                ),
                jnp.sum(grad_attn, axis=0, dtype=jnp.float32),
                jnp.sum(dpre, axis=0, dtype=jnp.float32),
                jnp.sum(grad_branch, axis=0, dtype=jnp.float32),
            ),
            "tok",
        )
        results.append((weight_parts, vector_parts))
    results = results[::-1]
    gain_grad = jnp.stack([item[1][0] for item in results])
    shift_grad = jnp.stack([item[1][1] for item in results])
    qkv_grad = jnp.stack([item[0][0] for item in results])
    qv_bias_grad = jnp.stack([item[1][2] for item in results])
    out_weight_grad = jnp.stack([item[0][1] for item in results])
    out_bias_grad = jnp.stack([item[1][3] for item in results])
    up_weight_grad = jnp.stack([item[0][2] for item in results])
    up_bias_grad = jnp.stack([item[1][4] for item in results])
    down_weight_grad = jnp.stack([item[0][3] for item in results])
    down_bias_grad = jnp.stack([item[1][5] for item in results])
    return (
        activations,
        grad_state,
        gain_grad,
        shift_grad,
        qkv_grad,
        qv_bias_grad,
        out_weight_grad,
        out_bias_grad,
        up_weight_grad,
        up_bias_grad,
        down_weight_grad,
        down_bias_grad,
    )


def solution(mesh):
    placed = (
        P("tok", "wid"),
        P("tok"),
        P(None, None, "wid"),
        P(None, None, "wid"),
        P(None, "tok", None, "wid"),
        P(None, None, "wid"),
        P(None, "wid", "tok"),
        P(None, "wid"),
        P(None, "tok", "wid"),
        P(None, "wid"),
        P(None, "wid", "tok"),
        P(None, "wid"),
        P("tok", "wid"),
    )
    return jax.shard_map(
        shards,
        mesh=mesh,
        in_specs=placed,
        out_specs=(
            P("tok", "wid"),
            P("tok", "wid"),
            P(None, None, "wid"),
            P(None, None, "wid"),
            P(None, "tok", None, "wid"),
            P(None, None, "wid"),
            P(None, "wid", "tok"),
            P(None, "wid"),
            P(None, "tok", "wid"),
            P(None, "wid"),
            P(None, "wid", "tok"),
            P(None, "wid"),
        ),
        check_vma=False,
    )
```

profile of v0, /device:TPU:0, one launch (start us, length us, event | category | flops | bytes accessed | tf_op | source)
XLA Modules:
  0.0 663.1 jit_solution(15200785847453675437)
XLA Ops:
  31.2 14.3 %all-to-all-done.1 = bf16[8,584,128]{2,1,0:T(8,128)(2,1)S(1)} async-done(((bf16[8,584,128]{2,1,0:T(8,128)(2,1)}), bf16[8,584,128]{2,1,0:T(8,128)(2,1)S(1)}, u32[]{:S(2)}, u32[]{:S(2)}) %all-to-all-start.1) | async-done | bytes 1196064 | tf_op jit(solution)/shard_map/all_to_all | solution.py:13
  47.1 17.8 %all-gather.3.cloned.1.call-done = bf16[1024,1536]{1,0:T(8,128)(2,1)} async-done(((bf16[64,1536]{1,0:T(8,128)(2,1)}), bf16[1024,1536]{1,0:T(8,128)(2,1)}) %all-gather.3.cloned.1.call-update) | async-done | bytes 3145744 | tf_op jit(solution)/shard_map/all_gather | solution.py:55
  81.5 16.7 %all-to-all-done.2 = bf16[8,584,128]{2,1,0:T(8,128)(2,1)} async-done(((bf16[8,584,128]{2,1,0:T(8,128)(2,1)}), bf16[8,584,128]{2,1,0:T(8,128)(2,1)}, u32[]{:S(2)}, u32[]{:S(2)}) %all-to-all-start.2) | async-done | bytes 1196064 | tf_op jit(solution)/shard_map/all_to_all | solution.py:48
  100.0 8.8 %all_to_all.140 = f32[8,1,1168]{2,1,0:T(1,128)S(1)} all-to-all(f32[8,1,1168]{2,1,0:T(1,128)S(1)} %broadcast_in_dim.120), channel_id=1, replica_groups=mesh['tok'=16,'wid'=8] {'wid'}, dimensions={0} | all-to-all | bytes 74752 | tf_op jit(solution)/shard_map/all_to_all | solution.py:13
  115.3 24.1 %all-to-all-done.4 = bf16[8,584,128]{2,1,0:T(8,128)(2,1)} async-done(((bf16[8,584,128]{2,1,0:T(8,128)(2,1)}), bf16[8,584,128]{2,1,0:T(8,128)(2,1)}, u32[]{:S(2)}, u32[]{:S(2)}) %all-to-all-start.4) | async-done | bytes 1196064 | tf_op jit(solution)/shard_map/all_to_all | solution.py:13
  153.9 15.8 %all-to-all-done.5 = bf16[8,584,128]{2,1,0:T(8,128)(2,1)} async-done(((bf16[8,584,128]{2,1,0:T(8,128)(2,1)}), bf16[8,584,128]{2,1,0:T(8,128)(2,1)}, u32[]{:S(2)}, u32[]{:S(2)}) %all-to-all-start.5) | async-done | bytes 1196064 | tf_op jit(solution)/shard_map/all_to_all | solution.py:48
  172.1 8.8 %all_to_all.141 = f32[8,1,1168]{2,1,0:T(1,128)S(1)} all-to-all(f32[8,1,1168]{2,1,0:T(1,128)S(1)} %broadcast_in_dim.122), channel_id=1, replica_groups=mesh['tok'=16,'wid'=8] {'wid'}, dimensions={0} | all-to-all | bytes 74752 | tf_op jit(solution)/shard_map/all_to_all | solution.py:13
  192.5 10.9 %all-to-all-done.7 = bf16[8,584,128]{2,1,0:T(8,128)(2,1)} async-done(((bf16[8,584,128]{2,1,0:T(8,128)(2,1)}), bf16[8,584,128]{2,1,0:T(8,128)(2,1)}, u32[]{:S(2)}, u32[]{:S(2)}) %all-to-all-start.7) | async-done | bytes 1196064 | tf_op jit(solution)/shard_map/all_to_all | solution.py:13
  225.0 17.7 %all_to_all.142 = bf16[8,584,128]{2,1,0:T(8,128)(2,1)S(1)} all-to-all(bf16[8,584,128]{2,1,0:T(8,128)(2,1)S(1)} %bitcast.374), channel_id=1, replica_groups=mesh['tok'=16,'wid'=8] {'wid'}, dimensions={0} | all-to-all | bytes 2392064 | tf_op jit(solution)/shard_map/all_to_all | solution.py:48
  244.7 8.7 %all_to_all.143 = f32[8,1,1168]{2,1,0:T(1,128)S(1)} all-to-all(f32[8,1,1168]{2,1,0:T(1,128)S(1)} %broadcast_in_dim.124), channel_id=1, replica_groups=mesh['tok'=16,'wid'=8] {'wid'}, dimensions={0} | all-to-all | bytes 74752 | tf_op jit(solution)/shard_map/all_to_all | solution.py:13
  254.9 16.3 %all_to_all.144 = bf16[8,584,128]{2,1,0:T(8,128)(2,1)} all-to-all(bf16[8,584,128]{2,1,0:T(8,128)(2,1)S(1)} %broadcast_in_dim.125), channel_id=1, replica_groups=mesh['tok'=16,'wid'=8] {'wid'}, dimensions={0} | all-to-all | bytes 2392064 | tf_op jit(solution)/shard_map/all_to_all | solution.py:13
  277.0 6.0 fusion.28
  283.0 6.8 %all-to-all-done.12 = bf16[8,584,128]{2,1,0:T(8,128)(2,1)} async-done(((bf16[8,584,128]{2,1,0:T(8,128)(2,1)}), bf16[8,584,128]{2,1,0:T(8,128)(2,1)}, u32[]{:S(2)}, u32[]{:S(2)}) %all-to-all-start.12) | async-done | bytes 1196064 | tf_op jit(solution)/shard_map/all_to_all | solution.py:13
  304.8 8.9 %all-to-all-done.13 = bf16[8,584,128]{2,1,0:T(8,128)(2,1)} async-done(((bf16[8,584,128]{2,1,0:T(8,128)(2,1)}), bf16[8,584,128]{2,1,0:T(8,128)(2,1)}, u32[]{:S(2)}, u32[]{:S(2)}) %all-to-all-start.13) | async-done | bytes 1196064 | tf_op jit(solution)/shard_map/all_to_all | solution.py:48
  321.6 8.9 %all-to-all-done.11 = bf16[8,584,128]{2,1,0:T(8,128)(2,1)} async-done(((bf16[8,584,128]{2,1,0:T(8,128)(2,1)}), bf16[8,584,128]{2,1,0:T(8,128)(2,1)}, u32[]{:S(2)}, u32[]{:S(2)}) %all-to-all-start.11) | async-done | bytes 1196064 | tf_op jit(solution)/shard_map/all_to_all | solution.py:48
  349.5 12.3 %all-to-all-done.15 = bf16[8,584,128]{2,1,0:T(8,128)(2,1)} async-done(((bf16[8,584,128]{2,1,0:T(8,128)(2,1)}), bf16[8,584,128]{2,1,0:T(8,128)(2,1)}, u32[]{:S(2)}, u32[]{:S(2)}) %all-to-all-start.15) | async-done | bytes 1196064 | tf_op jit(solution)/shard_map/all_to_all | solution.py:13
  376.4 15.1 %all_to_all.145 = bf16[8,584,128]{2,1,0:T(8,128)(2,1)S(1)} all-to-all(bf16[8,584,128]{2,1,0:T(8,128)(2,1)S(1)} %bitcast.375), channel_id=1, replica_groups=mesh['tok'=16,'wid'=8] {'wid'}, dimensions={0} | all-to-all | bytes 2392064 | tf_op jit(solution)/shard_map/all_to_all | solution.py:48
  393.2 8.8 %all_to_all.146 = f32[8,1,1168]{2,1,0:T(1,128)S(1)} all-to-all(f32[8,1,1168]{2,1,0:T(1,128)S(1)} %broadcast_in_dim.129), channel_id=1, replica_groups=mesh['tok'=16,'wid'=8] {'wid'}, dimensions={0} | all-to-all | bytes 74752 | tf_op jit(solution)/shard_map/all_to_all | solution.py:13
  410.3 12.3 %all-to-all-done.18 = bf16[8,584,128]{2,1,0:T(8,128)(2,1)} async-done(((bf16[8,584,128]{2,1,0:T(8,128)(2,1)}), bf16[8,584,128]{2,1,0:T(8,128)(2,1)}, u32[]{:S(2)}, u32[]{:S(2)}) %all-to-all-start.18) | async-done | bytes 1196064 | tf_op jit(solution)/shard_map/all_to_all | solution.py:13
  482.7 5.8 all-to-all-start.21
  555.4 16.9 %reduce-scatter.5.cloned.1.call-done = bf16[768,128]{1,0:T(8,128)(2,1)} async-done(((bf16[12288,128]{1,0:T(8,128)(2,1)}), bf16[768,128]{1,0:T(8,128)(2,1)}) %reduce-scatter.5.cloned.1.call-update) | async-done | bytes 196624 | tf_op jit(solution)/shard_map/reduce_scatter | solution.py:69
  581.5 6.2 all-to-all-done.23
  594.8 6.6 all-to-all-done.24
  605.0 45.5 %reduce-scatter.3.cloned.1.call-done = bf16[768,128]{1,0:T(8,128)(2,1)} async-done(((bf16[12288,128]{1,0:T(8,128)(2,1)}), bf16[768,128]{1,0:T(8,128)(2,1)}) %reduce-scatter.3.cloned.1.call-update) | async-done | bytes 196624 | tf_op jit(solution)/shard_map/reduce_scatter | solution.py:69
  (412 shorter events, 327.7 us)
Async XLA Ops:
  7.2 57.7 %all-gather.3.cloned.1.call-start = ((), (), s32[]{:S(2)}) async-start(), calls=%async_computation.28 | async-start | bytes 3342336 | tf_op jit(solution)/shard_map/all_gather | solution.py:55
  12.4 11.8 %all-to-all-start = ((f32[8,1,1168]{2,1,0:T(1,128)}), f32[8,1,1168]{2,1,0:T(1,128)S(1)}, u32[]{:S(2)}, u32[]{:S(2)}) async-start(f32[8,1,1168]{2,1,0:T(1,128)} %broadcast_in_dim.60), calls=%async_computation | async-start | bytes 81920 | tf_op jit(solution)/shard_map/all_to_all | solution.py:13
  18.4 162.6 %copy-start.41 = (f32[128]{0:T(128)}, f32[128]{0:T(128)S(1)}, u32[]{:S(2)}) copy-start(f32[128]{0:T(128)S(1)} %get-tuple-element.186) | copy-start | bytes 1540
  25.7 19.8 %all-to-all-start.1 = ((bf16[8,584,128]{2,1,0:T(8,128)(2,1)}), bf16[8,584,128]{2,1,0:T(8,128)(2,1)S(1)}, u32[]{:S(2)}, u32[]{:S(2)}) async-start(bf16[8,584,128]{2,1,0:T(8,128)(2,1)} %broadcast_in_dim.61), calls=%async_computation.1 | async-start | bytes 2392064 | tf_op jit(solution)/shard_map/all_to_all | solution.py:13
  75.7 22.4 %all-to-all-start.2 = ((bf16[8,584,128]{2,1,0:T(8,128)(2,1)}), bf16[8,584,128]{2,1,0:T(8,128)(2,1)}, u32[]{:S(2)}, u32[]{:S(2)}) async-start(bf16[8,584,128]{2,1,0:T(8,128)(2,1)} %bitcast.368), calls=%async_computation.2 | async-start | bytes 2392064 | tf_op jit(solution)/shard_map/all_to_all | solution.py:48
  80.2 107.8 %all-gather.5.cloned.1.call-start = ((), (), s32[]{:S(2)}) async-start(), calls=%async_computation.29 | async-start | bytes 3342336 | tf_op jit(solution)/shard_map/all_gather | solution.py:55
  110.4 29.1 %all-to-all-start.4 = ((bf16[8,584,128]{2,1,0:T(8,128)(2,1)}), bf16[8,584,128]{2,1,0:T(8,128)(2,1)}, u32[]{:S(2)}, u32[]{:S(2)}) async-start(bf16[8,584,128]{2,1,0:T(8,128)(2,1)} %broadcast_in_dim.121), calls=%async_computation.4 | async-start | bytes 2392064 | tf_op jit(solution)/shard_map/all_to_all | solution.py:13
  148.8 20.9 %all-to-all-start.5 = ((bf16[8,584,128]{2,1,0:T(8,128)(2,1)}), bf16[8,584,128]{2,1,0:T(8,128)(2,1)}, u32[]{:S(2)}, u32[]{:S(2)}) async-start(bf16[8,584,128]{2,1,0:T(8,128)(2,1)} %bitcast.373), calls=%async_computation.5 | async-start | bytes 2392064 | tf_op jit(solution)/shard_map/all_to_all | solution.py:48
  183.4 20.0 %all-to-all-start.7 = ((bf16[8,584,128]{2,1,0:T(8,128)(2,1)}), bf16[8,584,128]{2,1,0:T(8,128)(2,1)}, u32[]{:S(2)}, u32[]{:S(2)}) async-start(bf16[8,584,128]{2,1,0:T(8,128)(2,1)} %broadcast_in_dim.123), calls=%async_computation.7 | async-start | bytes 2392064 | tf_op jit(solution)/shard_map/all_to_all | solution.py:13
  272.4 17.4 %all-to-all-start.12 = ((bf16[8,584,128]{2,1,0:T(8,128)(2,1)}), bf16[8,584,128]{2,1,0:T(8,128)(2,1)}, u32[]{:S(2)}, u32[]{:S(2)}) async-start(bf16[8,584,128]{2,1,0:T(8,128)(2,1)} %broadcast_in_dim.126), calls=%async_computation.12 | async-start | bytes 2392064 | tf_op jit(solution)/shard_map/all_to_all | solution.py:13
  297.0 16.6 %all-to-all-start.13 = ((bf16[8,584,128]{2,1,0:T(8,128)(2,1)}), bf16[8,584,128]{2,1,0:T(8,128)(2,1)}, u32[]{:S(2)}, u32[]{:S(2)}) async-start(bf16[8,584,128]{2,1,0:T(8,128)(2,1)} %bitcast.372), calls=%async_computation.13 | async-start | bytes 2392064 | tf_op jit(solution)/shard_map/all_to_all | solution.py:48
  313.7 16.9 %all-to-all-start.11 = ((bf16[8,584,128]{2,1,0:T(8,128)(2,1)}), bf16[8,584,128]{2,1,0:T(8,128)(2,1)}, u32[]{:S(2)}, u32[]{:S(2)}) async-start(bf16[8,584,128]{2,1,0:T(8,128)(2,1)} %bitcast.370), calls=%async_computation.11 | async-start | bytes 2392064 | tf_op jit(solution)/shard_map/all_to_all | solution.py:48
  331.2 9.6 %all-to-all-start.14 = ((f32[8,1,1168]{2,1,0:T(1,128)}), f32[8,1,1168]{2,1,0:T(1,128)S(1)}, u32[]{:S(2)}, u32[]{:S(2)}) async-start(f32[8,1,1168]{2,1,0:T(1,128)} %broadcast_in_dim.127), calls=%async_computation.14 | async-start | bytes 81920 | tf_op jit(solution)/shard_map/all_to_all | solution.py:13
  344.9 16.8 %all-to-all-start.15 = ((bf16[8,584,128]{2,1,0:T(8,128)(2,1)}), bf16[8,584,128]{2,1,0:T(8,128)(2,1)}, u32[]{:S(2)}, u32[]{:S(2)}) async-start(bf16[8,584,128]{2,1,0:T(8,128)(2,1)} %broadcast_in_dim.128), calls=%async_computation.15 | async-start | bytes 2392064 | tf_op jit(solution)/shard_map/all_to_all | solution.py:13
  406.0 16.6 %all-to-all-start.18 = ((bf16[8,584,128]{2,1,0:T(8,128)(2,1)}), bf16[8,584,128]{2,1,0:T(8,128)(2,1)}, u32[]{:S(2)}, u32[]{:S(2)}) async-start(bf16[8,584,128]{2,1,0:T(8,128)(2,1)} %broadcast_in_dim.130), calls=%async_computation.18 | async-start | bytes 2392064 | tf_op jit(solution)/shard_map/all_to_all | solution.py:13
  429.2 26.0 %all-to-all-start.19 = ((bf16[8,584,128]{2,1,0:T(8,128)(2,1)}), bf16[8,584,128]{2,1,0:T(8,128)(2,1)}, u32[]{:S(2)}, u32[]{:S(2)}) async-start(bf16[8,584,128]{2,1,0:T(8,128)(2,1)} %bitcast.369), calls=%async_computation.19 | async-start | bytes 2392064 | tf_op jit(solution)/shard_map/all_to_all | solution.py:48
  459.2 19.4 %all-to-all-start.20 = ((f32[8,1,1168]{2,1,0:T(1,128)}), f32[8,1,1168]{2,1,0:T(1,128)S(1)}, u32[]{:S(2)}, u32[]{:S(2)}) async-start(f32[8,1,1168]{2,1,0:T(1,128)} %broadcast_in_dim.131), calls=%async_computation.20 | async-start | bytes 81920 | tf_op jit(solution)/shard_map/all_to_all | solution.py:13
  482.7 31.6 %all-to-all-start.21 = ((bf16[8,584,128]{2,1,0:T(8,128)(2,1)}), bf16[8,584,128]{2,1,0:T(8,128)(2,1)}, u32[]{:S(2)}, u32[]{:S(2)}) async-start(bf16[8,584,128]{2,1,0:T(8,128)(2,1)} %broadcast_in_dim.132), calls=%async_computation.21 | async-start | bytes 2392064 | tf_op jit(solution)/shard_map/all_to_all | solution.py:13
  488.5 83.8 %reduce-scatter.5.cloned.1.call-start = ((), (), s32[]{:S(2)}) async-start(), calls=%async_computation.31 | async-start | bytes 3342336 | tf_op jit(solution)/shard_map/reduce_scatter | solution.py:69
  495.9 154.5 %reduce-scatter.3.cloned.1.call-start = ((), (), s32[]{:S(2)}) async-start(), calls=%async_computation.30 | async-start | bytes 3342336 | tf_op jit(solution)/shard_map/reduce_scatter | solution.py:69
  538.0 11.5 %all-to-all-start.25 = ((f32[16,1,1536]{2,1,0:T(1,128)}), f32[16,1,1536]{2,1,0:T(1,128)S(1)}, u32[]{:S(2)}, u32[]{:S(2)}) async-start(f32[16,1,1536]{2,1,0:T(1,128)} %broadcast_in_dim.135), calls=%async_computation.25 | async-start | bytes 196608 | tf_op jit(solution)/shard_map/all_to_all | solution.py:13
  549.5 25.6 %all-to-all-start.22 = ((bf16[8,584,128]{2,1,0:T(8,128)(2,1)}), bf16[8,584,128]{2,1,0:T(8,128)(2,1)S(1)}, u32[]{:S(2)}, u32[]{:S(2)}) async-start(bf16[8,584,128]{2,1,0:T(8,128)(2,1)} %bitcast.351), calls=%async_computation.22 | async-start | bytes 2392064 | tf_op jit(solution)/shard_map/all_to_all | solution.py:48
  577.1 10.6 %all-to-all-start.23 = ((f32[8,1,1168]{2,1,0:T(1,128)}), f32[8,1,1168]{2,1,0:T(1,128)S(1)}, u32[]{:S(2)}, u32[]{:S(2)}) async-start(f32[8,1,1168]{2,1,0:T(1,128)} %broadcast_in_dim.133), calls=%async_computation.23 | async-start | bytes 81920 | tf_op jit(solution)/shard_map/all_to_all | solution.py:13
  588.4 13.0 %all-to-all-start.24 = ((f32[16,1,1536]{2,1,0:T(1,128)}), f32[16,1,1536]{2,1,0:T(1,128)S(1)}, u32[]{:S(2)}, u32[]{:S(2)}) async-start(f32[16,1,1536]{2,1,0:T(1,128)} %broadcast_in_dim.134), calls=%async_computation.24 | async-start | bytes 196608 | tf_op jit(solution)/shard_map/all_to_all | solution.py:13
  (72 other events, 488.7 us)
Sparse Core Ops, SparseCore 0:
  11.5 53.3 all-gather.2
  84.1 59.2 all-gather.4
  496.1 76.2 reduce-scatter.4
  576.3 74.1 reduce-scatter.2
where the time goes:
time: 676 us; the launch traced here: 663 us
  waiting for transfers between devices  238 us (35%)
  local copies, waits for them, and re-layouts  111 us (16%)
  starting transfers between devices  87.5 us (13%)
  blocking collectives  84.3 us (12%)
  matrix products  81.4 us (12%)
  other arithmetic  45.3 us (7%)
  between operations  15.3 us (2%)
    all_to_all x13, waiting for transfers between devices, copy_for_each(): return lax.all_to_all(copies, axis, split_axis=0, concat_axis=0, tiled=True)  108 us
    reduce_scatter x2, waiting for transfers between devices, sum_together(): lax.psum_scatter(lines, axis, tiled=True).reshape(-1)  62.4 us
    all_to_all x13, starting transfers between devices, copy_for_each(): return lax.all_to_all(copies, axis, split_axis=0, concat_axis=0, tiled=True)  59.3 us
    all_to_all x5, blocking collectives, copy_for_each(): return lax.all_to_all(copies, axis, split_axis=0, concat_axis=0, tiled=True)  51.4 us
    all_to_all x6, waiting for transfers between devices, summed_on_arrival(): lax.all_to_all(tiles, axis, split_axis=0, concat_axis=0, tiled=True)  50.2 us
    all_to_all x2, blocking collectives, summed_on_arrival(): lax.all_to_all(tiles, axis, split_axis=0, concat_axis=0, tiled=True)  32.8 us
    all_to_all x6, starting transfers between devices, summed_on_arrival(): lax.all_to_all(tiles, axis, split_axis=0, concat_axis=0, tiled=True)  27.9 us
    dot_general x8, matrix products, contract_rows(): lax.dot_general(left, right, (((0,), (0,)), ((), ())), preferred_element_...  23.1 us
  transfers between devices with their start and end apart: 23, of which 18 were waited for; matrix products, arithmetic and copies ran while one was open for 21% of the time, Pallas kernels for 0%

commit v1 on v0

--- a/solution.py
+++ b/solution.py
@@ -6,6 +6,13 @@
 HEAD = 64
 LAYERS = 2
 EPSILON = 1e-06
+
+
+def gather_over(shard, axis, dim):
+    size = lax.axis_size(axis)
+    parts = jnp.stack([shard for _ in range(size)])
+    parts = lax.all_to_all(parts, axis, split_axis=0, concat_axis=0)
+    return jnp.concatenate(parts, axis=dim)
 
 
 def copy_for_each(value, axis):
@@ -52,7 +59,7 @@
 def turned_gather(arrays, axis, dims):
     turned = [jnp.moveaxis(a, dim, 0) for a, dim in zip(arrays, dims)]
     both = jnp.concatenate([t.reshape(len(t), -1) for t in turned], axis=1)
-    filled, at, finished = (lax.all_gather(both, axis, axis=0, tiled=True), 0, [])
+    filled, at, finished = (gather_over(both, axis, 0), 0, [])
     for t, dim in zip(turned, dims):
         piece = filled[:, at : at + t[0].size].reshape(-1, *t.shape[1:])
         finished.append(jnp.moveaxis(piece, 0, dim))

time: 676 us -> 770 us (1.14)
  waiting for transfers between devices: 238 us -> 296 us
  starting transfers between devices: 87.5 us -> 117 us
  local copies, waits for them, and re-layouts: 111 us -> 126 us
    all_to_all x0 -> x2, waiting for transfers between devices: none -> 73.7 us  [gather_over(): parts = lax.all_to_all(parts, axis, split_axis=0, concat_axis=0)]
    all_to_all x0 -> x2, starting transfers between devices: none -> 18.4 us  [gather_over(): parts = lax.all_to_all(parts, axis, split_axis=0, concat_axis=0)]
    all_gather x2 -> x0, waiting for transfers between devices: 17.8 us -> none  [turned_gather(): lax.all_gather(both, axis, axis=0, tiled=True)]
    all_to_all x13 -> x14, starting transfers between devices: 59.3 us -> 70.3 us  [copy_for_each(): return lax.all_to_all(copies, axis, split_axis=0, concat_axis=0, tiled=True)]
    all_to_all x5 -> x4, blocking collectives: 51.4 us -> 45 us  [copy_for_each(): return lax.all_to_all(copies, axis, split_axis=0, concat_axis=0, tiled=True)]
    all_to_all x13 -> x14, waiting for transfers between devices: 108 us -> 106 us  [copy_for_each(): return lax.all_to_all(copies, axis, split_axis=0, concat_axis=0, tiled=True)]
  transfers between devices with their start and end apart: 23 -> 24, of which waited for: 18 -> 20; matrix products, arithmetic and copies ran while one was open for 21% -> 17% of each run, Pallas kernels for 0% -> 0%
where the time goes in v1:
time: 770 us; the launch traced here: 760 us
  waiting for transfers between devices  296 us (38%)
  local copies, waits for them, and re-layouts  126 us (16%)
  starting transfers between devices  117 us (15%)
  matrix products  80.2 us (10%)
  blocking collectives  80.1 us (10%)
  other arithmetic  45.5 us (6%)
  between operations  15.9 us (2%)
    all_to_all x14, waiting for transfers between devices, copy_for_each(): return lax.all_to_all(copies, axis, split_axis=0, concat_axis=0, tiled=True)  106 us
    all_to_all x2, waiting for transfers between devices, gather_over(): parts = lax.all_to_all(parts, axis, split_axis=0, concat_axis=0)  73.7 us
    all_to_all x14, starting transfers between devices, copy_for_each(): return lax.all_to_all(copies, axis, split_axis=0, concat_axis=0, tiled=True)  70.3 us
    reduce_scatter x2, waiting for transfers between devices, sum_together(): lax.psum_scatter(lines, axis, tiled=True).reshape(-1)  64.5 us
    all_to_all x6, waiting for transfers between devices, summed_on_arrival(): lax.all_to_all(tiles, axis, split_axis=0, concat_axis=0, tiled=True)  51.8 us
    all_to_all x4, blocking collectives, copy_for_each(): return lax.all_to_all(copies, axis, split_axis=0, concat_axis=0, tiled=True)  45 us
    all_to_all x2, blocking collectives, summed_on_arrival(): lax.all_to_all(tiles, axis, split_axis=0, concat_axis=0, tiled=True)  35.2 us
    all_to_all x6, starting transfers between devices, summed_on_arrival(): lax.all_to_all(tiles, axis, split_axis=0, concat_axis=0, tiled=True)  27.6 us
  transfers between devices with their start and end apart: 24, of which 20 were waited for; matrix products, arithmetic and copies ran while one was open for 17% of the time, Pallas kernels for 0%

profile of v1, /device:TPU:0, one launch (start us, length us, event | category | flops | bytes accessed | tf_op | source)
XLA Modules:
  0.0 759.9 jit_solution(13742780744946851022)
XLA Ops:
  30.2 13.5 %all-to-all-done.1 = bf16[8,584,128]{2,1,0:T(8,128)(2,1)S(1)} async-done(((bf16[8,584,128]{2,1,0:T(8,128)(2,1)}), bf16[8,584,128]{2,1,0:T(8,128)(2,1)S(1)}, u32[]{:S(2)}, u32[]{:S(2)}) %all-to-all-start.1) | async-done | bytes 1196064 | tf_op jit(solution)/shard_map/all_to_all | solution.py:20
  45.7 7.7 %all-to-all-start.2 = ((bf16[16,64,1536]{2,1,0:T(8,128)(2,1)}), bf16[16,64,1536]{2,1,0:T(8,128)(2,1)S(1)}, u32[]{:S(2)}, u32[]{:S(2)}) async-start(bf16[16,64,1536]{2,1,0:T(8,128)(2,1)} %stack.88), calls=%async_computation.2 | async-start | bytes 6291456 | tf_op jit(solution)/shard_map/all_to_all | solution.py:14
  60.2 34.8 %all-to-all-done.2 = bf16[16,64,1536]{2,1,0:T(8,128)(2,1)S(1)} async-done(((bf16[16,64,1536]{2,1,0:T(8,128)(2,1)}), bf16[16,64,1536]{2,1,0:T(8,128)(2,1)S(1)}, u32[]{:S(2)}, u32[]{:S(2)}) %all-to-all-start.2) | async-done | bytes 3145760 | tf_op jit(solution)/shard_map/all_to_all | solution.py:14
  114.9 16.8 %all-to-all-done.3 = bf16[8,584,128]{2,1,0:T(8,128)(2,1)} async-done(((bf16[8,584,128]{2,1,0:T(8,128)(2,1)}), bf16[8,584,128]{2,1,0:T(8,128)(2,1)}, u32[]{:S(2)}, u32[]{:S(2)}) %all-to-all-start.3) | async-done | bytes 1196064 | tf_op jit(solution)/shard_map/all_to_all | solution.py:55
  133.6 8.7 %all_to_all.152 = f32[8,1,1168]{2,1,0:T(1,128)S(1)} all-to-all(f32[8,1,1168]{2,1,0:T(1,128)S(1)} %broadcast_in_dim.120), channel_id=1, replica_groups=mesh['tok'=16,'wid'=8] {'wid'}, dimensions={0} | all-to-all | bytes 74752 | tf_op jit(solution)/shard_map/all_to_all | solution.py:20
  149.7 15.8 %all-to-all-done.5 = bf16[8,584,128]{2,1,0:T(8,128)(2,1)} async-done(((bf16[8,584,128]{2,1,0:T(8,128)(2,1)}), bf16[8,584,128]{2,1,0:T(8,128)(2,1)}, u32[]{:S(2)}, u32[]{:S(2)}) %all-to-all-start.5) | async-done | bytes 1196064 | tf_op jit(solution)/shard_map/all_to_all | solution.py:20
  179.7 14.9 %all-to-all-done.6 = bf16[8,584,128]{2,1,0:T(8,128)(2,1)} async-done(((bf16[8,584,128]{2,1,0:T(8,128)(2,1)}), bf16[8,584,128]{2,1,0:T(8,128)(2,1)}, u32[]{:S(2)}, u32[]{:S(2)}) %all-to-all-start.6) | async-done | bytes 1196064 | tf_op jit(solution)/shard_map/all_to_all | solution.py:55
  210.9 10.7 %all-to-all-start.9 = ((bf16[16,64,1536]{2,1,0:T(8,128)(2,1)}), bf16[16,64,1536]{2,1,0:T(8,128)(2,1)}, u32[]{:S(2)}, u32[]{:S(2)}) async-start(bf16[16,64,1536]{2,1,0:T(8,128)(2,1)} %stack.89), calls=%async_computation.9 | async-start | bytes 6291456 | tf_op jit(solution)/shard_map/all_to_all | solution.py:14
  224.3 38.9 %all-to-all-done.9 = bf16[16,64,1536]{2,1,0:T(8,128)(2,1)} async-done(((bf16[16,64,1536]{2,1,0:T(8,128)(2,1)}), bf16[16,64,1536]{2,1,0:T(8,128)(2,1)}, u32[]{:S(2)}, u32[]{:S(2)}) %all-to-all-start.9) | async-done | bytes 3145760 | tf_op jit(solution)/shard_map/all_to_all | solution.py:14
  274.4 12.7 %all-to-all-done.8 = bf16[8,584,128]{2,1,0:T(8,128)(2,1)} async-done(((bf16[8,584,128]{2,1,0:T(8,128)(2,1)}), bf16[8,584,128]{2,1,0:T(8,128)(2,1)}, u32[]{:S(2)}, u32[]{:S(2)}) %all-to-all-start.8) | async-done | bytes 1196064 | tf_op jit(solution)/shard_map/all_to_all | solution.py:20
  308.7 20.0 %all_to_all.153 = bf16[8,584,128]{2,1,0:T(8,128)(2,1)S(1)} all-to-all(bf16[8,584,128]{2,1,0:T(8,128)(2,1)S(1)} %bitcast.384), channel_id=1, replica_groups=mesh['tok'=16,'wid'=8] {'wid'}, dimensions={0} | all-to-all | bytes 2392064 | tf_op jit(solution)/shard_map/all_to_all | solution.py:55
  330.8 8.7 %all_to_all.154 = f32[8,1,1168]{2,1,0:T(1,128)S(1)} all-to-all(f32[8,1,1168]{2,1,0:T(1,128)S(1)} %broadcast_in_dim.124), channel_id=1, replica_groups=mesh['tok'=16,'wid'=8] {'wid'}, dimensions={0} | all-to-all | bytes 74752 | tf_op jit(solution)/shard_map/all_to_all | solution.py:20
  341.0 18.8 %all_to_all.155 = bf16[8,584,128]{2,1,0:T(8,128)(2,1)} all-to-all(bf16[8,584,128]{2,1,0:T(8,128)(2,1)S(1)} %broadcast_in_dim.125), channel_id=1, replica_groups=mesh['tok'=16,'wid'=8] {'wid'}, dimensions={0} | all-to-all | bytes 2392064 | tf_op jit(solution)/shard_map/all_to_all | solution.py:20
  371.8 8.2 %all-to-all-done.14 = bf16[8,584,128]{2,1,0:T(8,128)(2,1)} async-done(((bf16[8,584,128]{2,1,0:T(8,128)(2,1)}), bf16[8,584,128]{2,1,0:T(8,128)(2,1)}, u32[]{:S(2)}, u32[]{:S(2)}) %all-to-all-start.14) | async-done | bytes 1196064 | tf_op jit(solution)/shard_map/all_to_all | solution.py:20
  394.4 9.8 %all-to-all-done.15 = bf16[8,584,128]{2,1,0:T(8,128)(2,1)} async-done(((bf16[8,584,128]{2,1,0:T(8,128)(2,1)}), bf16[8,584,128]{2,1,0:T(8,128)(2,1)}, u32[]{:S(2)}, u32[]{:S(2)}) %all-to-all-start.15) | async-done | bytes 1196064 | tf_op jit(solution)/shard_map/all_to_all | solution.py:55
  411.4 10.3 %all-to-all-done.13 = bf16[8,584,128]{2,1,0:T(8,128)(2,1)} async-done(((bf16[8,584,128]{2,1,0:T(8,128)(2,1)}), bf16[8,584,128]{2,1,0:T(8,128)(2,1)}, u32[]{:S(2)}, u32[]{:S(2)}) %all-to-all-start.13) | async-done | bytes 1196064 | tf_op jit(solution)/shard_map/all_to_all | solution.py:55
  440.5 12.3 %all-to-all-done.17 = bf16[8,584,128]{2,1,0:T(8,128)(2,1)} async-done(((bf16[8,584,128]{2,1,0:T(8,128)(2,1)}), bf16[8,584,128]{2,1,0:T(8,128)(2,1)}, u32[]{:S(2)}, u32[]{:S(2)}) %all-to-all-start.17) | async-done | bytes 1196064 | tf_op jit(solution)/shard_map/all_to_all | solution.py:20
  466.8 15.1 %all_to_all.156 = bf16[8,584,128]{2,1,0:T(8,128)(2,1)S(1)} all-to-all(bf16[8,584,128]{2,1,0:T(8,128)(2,1)S(1)} %bitcast.385), channel_id=1, replica_groups=mesh['tok'=16,'wid'=8] {'wid'}, dimensions={0} | all-to-all | bytes 2392064 | tf_op jit(solution)/shard_map/all_to_all | solution.py:55
  483.6 8.7 %all_to_all.157 = f32[8,1,1168]{2,1,0:T(1,128)S(1)} all-to-all(f32[8,1,1168]{2,1,0:T(1,128)S(1)} %broadcast_in_dim.129), channel_id=1, replica_groups=mesh['tok'=16,'wid'=8] {'wid'}, dimensions={0} | all-to-all | bytes 74752 | tf_op jit(solution)/shard_map/all_to_all | solution.py:20
  500.7 12.3 %all-to-all-done.20 = bf16[8,584,128]{2,1,0:T(8,128)(2,1)} async-done(((bf16[8,584,128]{2,1,0:T(8,128)(2,1)}), bf16[8,584,128]{2,1,0:T(8,128)(2,1)}, u32[]{:S(2)}, u32[]{:S(2)}) %all-to-all-start.20) | async-done | bytes 1196064 | tf_op jit(solution)/shard_map/all_to_all | solution.py:20
  625.3 10.3 %all-to-all-start.27 = ((f32[16,1,1536]{2,1,0:T(1,128)}), f32[16,1,1536]{2,1,0:T(1,128)S(1)}, u32[]{:S(2)}, u32[]{:S(2)}) async-start(f32[16,1,1536]{2,1,0:T(1,128)} %broadcast_in_dim.135), calls=%async_computation.27 | async-start | bytes 196608 | tf_op jit(solution)/shard_map/all_to_all | solution.py:20
  649.4 19.0 %reduce-scatter.5.cloned.1.call-done = bf16[768,128]{1,0:T(8,128)(2,1)} async-done(((bf16[12288,128]{1,0:T(8,128)(2,1)}), bf16[768,128]{1,0:T(8,128)(2,1)}) %reduce-scatter.5.cloned.1.call-update) | async-done | bytes 196624 | tf_op jit(solution)/shard_map/reduce_scatter | solution.py:76
  691.0 6.6 all-to-all-done.26
  701.1 45.6 %reduce-scatter.3.cloned.1.call-done = bf16[768,128]{1,0:T(8,128)(2,1)} async-done(((bf16[12288,128]{1,0:T(8,128)(2,1)}), bf16[768,128]{1,0:T(8,128)(2,1)}) %reduce-scatter.3.cloned.1.call-update) | async-done | bytes 196624 | tf_op jit(solution)/shard_map/reduce_scatter | solution.py:76
  (435 shorter events, 363.8 us)
Async XLA Ops:
  9.0 11.8 %all-to-all-start = ((f32[8,1,1168]{2,1,0:T(1,128)}), f32[8,1,1168]{2,1,0:T(1,128)S(1)}, u32[]{:S(2)}, u32[]{:S(2)}) async-start(f32[8,1,1168]{2,1,0:T(1,128)} %broadcast_in_dim.60), calls=%async_computation | async-start | bytes 81920 | tf_op jit(solution)/shard_map/all_to_all | solution.py:20
  23.8 19.8 %all-to-all-start.1 = ((bf16[8,584,128]{2,1,0:T(8,128)(2,1)}), bf16[8,584,128]{2,1,0:T(8,128)(2,1)S(1)}, u32[]{:S(2)}, u32[]{:S(2)}) async-start(bf16[8,584,128]{2,1,0:T(8,128)(2,1)} %broadcast_in_dim.61), calls=%async_computation.1 | async-start | bytes 2392064 | tf_op jit(solution)/shard_map/all_to_all | solution.py:20
  45.7 49.3 %all-to-all-start.2 = ((bf16[16,64,1536]{2,1,0:T(8,128)(2,1)}), bf16[16,64,1536]{2,1,0:T(8,128)(2,1)S(1)}, u32[]{:S(2)}, u32[]{:S(2)}) async-start(bf16[16,64,1536]{2,1,0:T(8,128)(2,1)} %stack.88), calls=%async_computation.2 | async-start | bytes 6291456 | tf_op jit(solution)/shard_map/all_to_all | solution.py:14
  110.0 21.8 %all-to-all-start.3 = ((bf16[8,584,128]{2,1,0:T(8,128)(2,1)}), bf16[8,584,128]{2,1,0:T(8,128)(2,1)}, u32[]{:S(2)}, u32[]{:S(2)}) async-start(bf16[8,584,128]{2,1,0:T(8,128)(2,1)} %bitcast.383), calls=%async_computation.3 | async-start | bytes 2392064 | tf_op jit(solution)/shard_map/all_to_all | solution.py:55
  144.5 21.0 %all-to-all-start.5 = ((bf16[8,584,128]{2,1,0:T(8,128)(2,1)}), bf16[8,584,128]{2,1,0:T(8,128)(2,1)}, u32[]{:S(2)}, u32[]{:S(2)}) async-start(bf16[8,584,128]{2,1,0:T(8,128)(2,1)} %broadcast_in_dim.121), calls=%async_computation.5 | async-start | bytes 2392064 | tf_op jit(solution)/shard_map/all_to_all | solution.py:20
  174.7 19.9 %all-to-all-start.6 = ((bf16[8,584,128]{2,1,0:T(8,128)(2,1)}), bf16[8,584,128]{2,1,0:T(8,128)(2,1)}, u32[]{:S(2)}, u32[]{:S(2)}) async-start(bf16[8,584,128]{2,1,0:T(8,128)(2,1)} %bitcast.381), calls=%async_computation.6 | async-start | bytes 2392064 | tf_op jit(solution)/shard_map/all_to_all | solution.py:55
  197.7 10.3 %all-to-all-start.7 = ((f32[8,1,1168]{2,1,0:T(1,128)}), f32[8,1,1168]{2,1,0:T(1,128)}, u32[]{:S(2)}, u32[]{:S(2)}) async-start(f32[8,1,1168]{2,1,0:T(1,128)} %broadcast_in_dim.122), calls=%async_computation.7 | async-start | bytes 81920 | tf_op jit(solution)/shard_map/all_to_all | solution.py:20
  210.9 52.3 %all-to-all-start.9 = ((bf16[16,64,1536]{2,1,0:T(8,128)(2,1)}), bf16[16,64,1536]{2,1,0:T(8,128)(2,1)}, u32[]{:S(2)}, u32[]{:S(2)}) async-start(bf16[16,64,1536]{2,1,0:T(8,128)(2,1)} %stack.89), calls=%async_computation.9 | async-start | bytes 6291456 | tf_op jit(solution)/shard_map/all_to_all | solution.py:14
  265.4 21.8 %all-to-all-start.8 = ((bf16[8,584,128]{2,1,0:T(8,128)(2,1)}), bf16[8,584,128]{2,1,0:T(8,128)(2,1)}, u32[]{:S(2)}, u32[]{:S(2)}) async-start(bf16[8,584,128]{2,1,0:T(8,128)(2,1)} %broadcast_in_dim.123), calls=%async_computation.8 | async-start | bytes 2392064 | tf_op jit(solution)/shard_map/all_to_all | solution.py:20
  361.0 19.0 %all-to-all-start.14 = ((bf16[8,584,128]{2,1,0:T(8,128)(2,1)}), bf16[8,584,128]{2,1,0:T(8,128)(2,1)}, u32[]{:S(2)}, u32[]{:S(2)}) async-start(bf16[8,584,128]{2,1,0:T(8,128)(2,1)} %broadcast_in_dim.126), calls=%async_computation.14 | async-start | bytes 2392064 | tf_op jit(solution)/shard_map/all_to_all | solution.py:20
  386.6 17.6 %all-to-all-start.15 = ((bf16[8,584,128]{2,1,0:T(8,128)(2,1)}), bf16[8,584,128]{2,1,0:T(8,128)(2,1)}, u32[]{:S(2)}, u32[]{:S(2)}) async-start(bf16[8,584,128]{2,1,0:T(8,128)(2,1)} %bitcast.382), calls=%async_computation.15 | async-start | bytes 2392064 | tf_op jit(solution)/shard_map/all_to_all | solution.py:55
  404.2 17.5 %all-to-all-start.13 = ((bf16[8,584,128]{2,1,0:T(8,128)(2,1)}), bf16[8,584,128]{2,1,0:T(8,128)(2,1)}, u32[]{:S(2)}, u32[]{:S(2)}) async-start(bf16[8,584,128]{2,1,0:T(8,128)(2,1)} %bitcast.380), calls=%async_computation.13 | async-start | bytes 2392064 | tf_op jit(solution)/shard_map/all_to_all | solution.py:55
  422.3 9.6 %all-to-all-start.16 = ((f32[8,1,1168]{2,1,0:T(1,128)}), f32[8,1,1168]{2,1,0:T(1,128)S(1)}, u32[]{:S(2)}, u32[]{:S(2)}) async-start(f32[8,1,1168]{2,1,0:T(1,128)} %broadcast_in_dim.127), calls=%async_computation.16 | async-start | bytes 81920 | tf_op jit(solution)/shard_map/all_to_all | solution.py:20
  436.0 16.8 %all-to-all-start.17 = ((bf16[8,584,128]{2,1,0:T(8,128)(2,1)}), bf16[8,584,128]{2,1,0:T(8,128)(2,1)}, u32[]{:S(2)}, u32[]{:S(2)}) async-start(bf16[8,584,128]{2,1,0:T(8,128)(2,1)} %broadcast_in_dim.128), calls=%async_computation.17 | async-start | bytes 2392064 | tf_op jit(solution)/shard_map/all_to_all | solution.py:20
  496.4 16.6 %all-to-all-start.20 = ((bf16[8,584,128]{2,1,0:T(8,128)(2,1)}), bf16[8,584,128]{2,1,0:T(8,128)(2,1)}, u32[]{:S(2)}, u32[]{:S(2)}) async-start(bf16[8,584,128]{2,1,0:T(8,128)(2,1)} %broadcast_in_dim.130), calls=%async_computation.20 | async-start | bytes 2392064 | tf_op jit(solution)/shard_map/all_to_all | solution.py:20
  519.7 25.9 %all-to-all-start.21 = ((bf16[8,584,128]{2,1,0:T(8,128)(2,1)}), bf16[8,584,128]{2,1,0:T(8,128)(2,1)}, u32[]{:S(2)}, u32[]{:S(2)}) async-start(bf16[8,584,128]{2,1,0:T(8,128)(2,1)} %bitcast.379), calls=%async_computation.21 | async-start | bytes 2392064 | tf_op jit(solution)/shard_map/all_to_all | solution.py:55
  549.6 19.4 %all-to-all-start.22 = ((f32[8,1,1168]{2,1,0:T(1,128)}), f32[8,1,1168]{2,1,0:T(1,128)S(1)}, u32[]{:S(2)}, u32[]{:S(2)}) async-start(f32[8,1,1168]{2,1,0:T(1,128)} %broadcast_in_dim.131), calls=%async_computation.22 | async-start | bytes 81920 | tf_op jit(solution)/shard_map/all_to_all | solution.py:20
  572.5 31.6 %all-to-all-start.23 = ((bf16[8,584,128]{2,1,0:T(8,128)(2,1)}), bf16[8,584,128]{2,1,0:T(8,128)(2,1)}, u32[]{:S(2)}, u32[]{:S(2)}) async-start(bf16[8,584,128]{2,1,0:T(8,128)(2,1)} %broadcast_in_dim.132), calls=%async_computation.23 | async-start | bytes 2392064 | tf_op jit(solution)/shard_map/all_to_all | solution.py:20
  578.4 90.0 %reduce-scatter.5.cloned.1.call-start = ((), (), s32[]{:S(2)}) async-start(), calls=%async_computation.31 | async-start | bytes 3342336 | tf_op jit(solution)/shard_map/reduce_scatter | solution.py:76
  585.8 160.9 %reduce-scatter.3.cloned.1.call-start = ((), (), s32[]{:S(2)}) async-start(), calls=%async_computation.30 | async-start | bytes 3342336 | tf_op jit(solution)/shard_map/reduce_scatter | solution.py:76
  625.3 18.1 %all-to-all-start.27 = ((f32[16,1,1536]{2,1,0:T(1,128)}), f32[16,1,1536]{2,1,0:T(1,128)S(1)}, u32[]{:S(2)}, u32[]{:S(2)}) async-start(f32[16,1,1536]{2,1,0:T(1,128)} %broadcast_in_dim.135), calls=%async_computation.27 | async-start | bytes 196608 | tf_op jit(solution)/shard_map/all_to_all | solution.py:20
  643.4 27.7 %all-to-all-start.24 = ((bf16[8,584,128]{2,1,0:T(8,128)(2,1)}), bf16[8,584,128]{2,1,0:T(8,128)(2,1)S(1)}, u32[]{:S(2)}, u32[]{:S(2)}) async-start(bf16[8,584,128]{2,1,0:T(8,128)(2,1)} %bitcast.353), calls=%async_computation.24 | async-start | bytes 2392064 | tf_op jit(solution)/shard_map/all_to_all | solution.py:55
  673.1 10.6 %all-to-all-start.25 = ((f32[8,1,1168]{2,1,0:T(1,128)}), f32[8,1,1168]{2,1,0:T(1,128)S(1)}, u32[]{:S(2)}, u32[]{:S(2)}) async-start(f32[8,1,1168]{2,1,0:T(1,128)} %broadcast_in_dim.133), calls=%async_computation.25 | async-start | bytes 81920 | tf_op jit(solution)/shard_map/all_to_all | solution.py:20
  684.4 13.2 %all-to-all-start.26 = ((f32[16,1,1536]{2,1,0:T(1,128)}), f32[16,1,1536]{2,1,0:T(1,128)S(1)}, u32[]{:S(2)}, u32[]{:S(2)}) async-start(f32[16,1,1536]{2,1,0:T(1,128)} %broadcast_in_dim.134), calls=%async_computation.26 | async-start | bytes 196608 | tf_op jit(solution)/shard_map/all_to_all | solution.py:20
  (84 other events, 700.4 us)
Sparse Core Ops, SparseCore 0:
  585.9 82.4 reduce-scatter.4
  672.5 74.1 reduce-scatter.2
